TPU v7x, 32 devices: a whole 2x2x4 slice. The times are simulated.
32 devices in a mesh: ctx: 8 (over z, y), tp: 4 (over x, core).
Axes of the slice: x: 2, y: 2, z: 4, core: 2. Of those that a mesh axis runs over, the one named last changes fastest.
Arguments:
- qkv: bfloat16 [1024, 3, 8192], P(('ctx', 'tp')), may hold values from -6 to 6
- filters: float32 [3, 7, 8192], P(None, None, 'tp'), may hold values from -1.5 to 1.5
- doc_ids: int32 [8], replicated, may hold values from 0 to 1, never falling along the last dimension, each value on 1 to 5 neighbouring positions
- upstream: bfloat16 [1024, 8192], P('ctx', 'tp'), may hold values from -6 to 6
Outputs:
- attended: bfloat16 [1024, 8192], P('ctx', 'tp')
- qkv_grad: bfloat16 [1024, 3, 8192], P(('ctx', 'tp'))
- filter_grad: float32 [3, 7, 8192], P(None, None, 'tp')
Inputs may be any that keep to these rules, and one draw needn't show every extreme that they name: doc_ids never falls along the sequence; every document covers 1 to 5 whole blocks of 128 tokens.
All inputs are finite; a program needn't handle non-finite values.
Results may differ from a plain program's by a relative error of at most 0.014.
The roundings to bfloat16 on the way count: a program that leaves them out, or rounds other values in their place, can miss the bound.
Values may be sent and summed in bfloat16 or wider, within the bound.
No kernel may reach another device: no remote copies, remote signals or barrier semaphores. Data moves between devices by JAX's collectives and lax.ppermute only.
A program may use at most 128 MiB of HBM per device.

v0:
```python
import jax
import jax.numpy as jnp
from jax import lax
from jax.sharding import PartitionSpec as P

HEAD_DIM = 128
KW = 7
BLOCK = 128
STEPS = 4


def from_behind(value, axis, steps):
    count = lax.axis_size(axis)
    first, last = (max(0, -steps), min(count, count - steps))
    return lax.ppermute(value, axis, [(source, source + steps) for source in range(first, last)])


def block_docs(doc_ids, first_block, count):
    start = jnp.maximum(first_block, 0)
    picked = lax.dynamic_slice_in_dim(doc_ids, start, count)
    return jnp.repeat(picked, BLOCK)


def shards(qkv, filters, doc_ids, upstream):
    local = lax.all_to_all(qkv, "tp", split_axis=2, concat_axis=0, tiled=True)
    tokens = local.shape[0]
    width = local.shape[2]
    heads = width // HEAD_DIM
    blocks_here = tokens // BLOCK
    logit_scale = HEAD_DIM ** (-0.5)
    position = lax.axis_index("ctx")
    reach = STEPS + 1
    rim = from_behind(local[tokens - (KW - 1) :], "ctx", 1)
    inputs = jnp.concatenate([rim, local], axis=0).astype(jnp.float32)
    mixed = sum(
        (filters[:, lag, :] * inputs[KW - 1 - lag : KW - 1 - lag + tokens] for lag in range(KW))
    )
    mixed = mixed.astype(jnp.bfloat16)
    queries = mixed[:, 0].reshape(tokens, heads, HEAD_DIM)
    key_value = mixed[:, 1:3]
    tiles = [key_value]
    current = key_value
    for distance in range(1, STEPS + 1):
        current = from_behind(current, "ctx", 1)
        tiles.append(current)
    joined = jnp.concatenate(tiles, axis=0)
    keys = joined[:, 0].reshape(reach * tokens, heads, HEAD_DIM)
    values = joined[:, 1].reshape(reach * tokens, heads, HEAD_DIM)
    rows = jnp.arange(tokens)
    query_token = position * tokens + rows
    query_doc = block_docs(doc_ids, position * blocks_here, blocks_here)
    key_tokens = jnp.concatenate(
        [(position - distance) * tokens + rows for distance in range(reach)]
    )
    key_docs = jnp.concatenate(
        [
            block_docs(doc_ids, (position - distance) * blocks_here, blocks_here)
            for distance in range(reach)
        ]
    )
    allowed = (
        (key_tokens[None, :] >= 0)
        & (key_tokens[None, :] <= query_token[:, None])
        & (key_docs[None, :] == query_doc[:, None])
    )
    raw = (
        jnp.einsum("qhd,khd->hqk", queries, keys, preferred_element_type=jnp.float32) * logit_scale
    )
    masked = jnp.where(allowed[None], raw, -1e30)
    row_max = masked.max(axis=2)
    expo = jnp.where(allowed[None], jnp.exp(masked - row_max[:, :, None]), 0.0)
    row_sum = expo.sum(axis=2)
    weighted_values = jnp.einsum(
        "hqk,khd->qhd", expo.astype(jnp.bfloat16), values, preferred_element_type=jnp.float32
    )
    attended = (weighted_values / row_sum.T[:, :, None]).astype(jnp.bfloat16)
    grad_out = upstream.reshape(tokens, heads, HEAD_DIM)
    delta = jnp.sum(grad_out.astype(jnp.float32) * attended.astype(jnp.float32), axis=-1).T
    prob = expo / row_sum[:, :, None]
    value_part = jnp.einsum(
        "hqk,qhd->khd", prob.astype(jnp.bfloat16), grad_out, preferred_element_type=jnp.float32
    )
    probability_gradient = jnp.einsum(
        "qhd,khd->hqk", grad_out, values, preferred_element_type=jnp.float32
    )
    score_gradient = (prob * (probability_gradient - delta[:, :, None]) * logit_scale).astype(
        jnp.bfloat16
    )
    query_gradient_rows = jnp.einsum(
        "hqk,khd->qhd", score_gradient, keys, preferred_element_type=jnp.float32
    )
    key_part = jnp.einsum(
        "hqk,qhd->khd", score_gradient, queries, preferred_element_type=jnp.float32
    )
    stacked = jnp.stack(
        [key_part.reshape(reach, tokens, width), value_part.reshape(reach, tokens, width)], axis=2
    )
    partials = [stacked[distance] for distance in range(reach)]
    carried = partials[STEPS]
    for distance in range(STEPS - 1, -1, -1):
        carried = from_behind(carried, "ctx", -1)
        carried = carried + partials[distance]
    conv_grad = jnp.concatenate([query_gradient_rows.reshape(tokens, 1, width), carried], axis=1)
    grad_edge = from_behind(conv_grad[: KW - 1], "ctx", -1)
    extended = jnp.concatenate([conv_grad, grad_edge], axis=0)
    input_grad = sum((filters[:, lag, :] * extended[lag : lag + tokens] for lag in range(KW)))
    tap_terms = jnp.stack(
        [
            jnp.sum(inputs[KW - 1 - lag : KW - 1 - lag + tokens] * conv_grad, axis=0)
            for lag in range(KW)
        ],
        axis=1,
    )
    filter_grad = lax.psum(tap_terms, "ctx")
    qkv_grad = lax.all_to_all(
        input_grad.astype(jnp.bfloat16), "tp", split_axis=0, concat_axis=2, tiled=True
    )
    return (attended.reshape(tokens, width), qkv_grad, filter_grad)


def solution(mesh):
    return jax.shard_map(
        shards,
        mesh=mesh,
        in_specs=(P(("ctx", "tp"), None, None), P(None, None, "tp"), P(), P("ctx", "tp")),
        out_specs=(P("ctx", "tp"), P(("ctx", "tp"), None, None), P(None, None, "tp")),
        check_vma=False,
    )
```

profile of v0, /device:TPU:0, one launch (start us, length us, event | category | flops | bytes accessed | tf_op | source)
XLA Modules:
  0.0 541.6 jit_solution(776772498163065581)
XLA Ops:
  7.2 10.7 %copy.57 = bf16[32,3,8192]{0,1,2:T(4,128)(2,1)} copy(bf16[32,3,8192]{2,0,1:T(8,128)(2,1)} %param.4) | data formatting | bytes 3145728 | tf_op args[0]
  17.8 8.4 %reshape.158 = bf16[4,2,98304]{2,1,0:T(2,128)(2,1)} reshape(bf16[8192,3,32]{2,1,0:T(4,128)(2,1)} %bitcast.114) | data formatting | bytes 3145728
  30.7 19.9 %all-to-all-done = bf16[4,2,98304]{2,1,0:T(2,128)(2,1)S(1)} async-done(((bf16[4,2,98304]{2,1,0:T(2,128)(2,1)}), bf16[4,2,98304]{2,1,0:T(2,128)(2,1)S(1)}, u32[]{:S(2)}, u32[]{:S(2)}) %all-to-all-start) | async-done | bytes 1572896 | tf_op jit(solution)/shard_map/all_to_all | solution.py:25
  50.6 7.1 %reshape.159 = bf16[8192,3,32]{2,1,0:T(4,128)(2,1)} reshape(bf16[4,2,98304]{2,1,0:T(2,128)(2,1)S(1)} %all-to-all-done) | data formatting | bytes 3145728
  57.7 10.5 %copy.59 = bf16[4,32,3,2048]{3,1,0,2:T(8,128)(2,1)S(1)} copy(bf16[4,32,3,2048]{1,2,3,0:T(4,128)(2,1)} %bitcast.113) | data formatting | bytes 3145728 | tf_op jit(solution)/shard_map/all_to_all | solution.py:25
  81.5 5.3 collective-permute-start.1
  86.8 20.0 %collective-permute-done.1 = bf16[128,2,2048]{2,0,1:T(8,128)(2,1)} collective-permute-done((bf16[128,2,2048]{2,0,1:T(8,128)(2,1)S(1)}, bf16[128,2,2048]{2,0,1:T(8,128)(2,1)}, u32[]{:S(2)}, u32[]{:S(2)}) %collective-permute-start.1) | collective-permute-done | bytes 1048608 | tf_op jit(solution)/shard_map/ppermute | solution.py:15
  106.8 5.5 %collective-permute-start.2 = (bf16[128,2,2048]{2,0,1:T(8,128)(2,1)}, bf16[128,2,2048]{2,0,1:T(8,128)(2,1)}, u32[]{:S(2)}, u32[]{:S(2)}) collective-permute-start(bf16[128,2,2048]{2,0,1:T(8,128)(2,1)} %collective-permute-done.1), channel_id=1, source_target_pairs={{0,4},{4,8},{8,12},{12,16},{16,20},{20,24},{24,28},{1,5},{5,9},{9,... | collective-permute-start | bytes 3145736 | tf_op jit(solution)/shard_map/ppermute | solution.py:15
  112.8 19.0 %collective-permute-done.2 = bf16[128,2,2048]{2,0,1:T(8,128)(2,1)} collective-permute-done((bf16[128,2,2048]{2,0,1:T(8,128)(2,1)}, bf16[128,2,2048]{2,0,1:T(8,128)(2,1)}, u32[]{:S(2)}, u32[]{:S(2)}) %collective-permute-start.2) | collective-permute-done | bytes 1048608 | tf_op jit(solution)/shard_map/ppermute | solution.py:15
  131.8 6.2 %collective-permute-start.3 = (bf16[128,2,2048]{2,0,1:T(8,128)(2,1)}, bf16[128,2,2048]{2,0,1:T(8,128)(2,1)}, u32[]{:S(2)}, u32[]{:S(2)}) collective-permute-start(bf16[128,2,2048]{2,0,1:T(8,128)(2,1)} %collective-permute-done.2), channel_id=1, source_target_pairs={{0,4},{4,8},{8,12},{12,16},{16,20},{20,24},{24,28},{1,5},{5,9},{9,... | collective-permute-start | bytes 3145736 | tf_op jit(solution)/shard_map/ppermute | solution.py:15
  141.8 14.7 %collective-permute-done.3 = bf16[128,2,2048]{2,0,1:T(8,128)(2,1)} collective-permute-done((bf16[128,2,2048]{2,0,1:T(8,128)(2,1)}, bf16[128,2,2048]{2,0,1:T(8,128)(2,1)}, u32[]{:S(2)}, u32[]{:S(2)}) %collective-permute-start.3) | collective-permute-done | bytes 1048608 | tf_op jit(solution)/shard_map/ppermute | solution.py:15
  156.5 6.3 %collective-permute-start.4 = (bf16[128,2,2048]{2,0,1:T(8,128)(2,1)}, bf16[128,2,2048]{2,0,1:T(8,128)(2,1)}, u32[]{:S(2)}, u32[]{:S(2)}) collective-permute-start(bf16[128,2,2048]{2,0,1:T(8,128)(2,1)} %collective-permute-done.3), channel_id=1, source_target_pairs={{0,4},{4,8},{8,12},{12,16},{16,20},{20,24},{24,28},{1,5},{5,9},{9,... | collective-permute-start | bytes 3145736 | tf_op jit(solution)/shard_map/ppermute | solution.py:15
  182.7 5.7 %fusion.48 = (bf16[640,1,2048]{2,0,1:T(8,128)(2,1)}, bf16[640,1,2048]{2,0,1:T(8,128)(2,1)}) fusion(bf16[640,2,2048]{2,0,1:T(8,128)(2,1)} %constant_dynamic-update-slice_fusion), kind=kLoop, calls=%fused_computation.106 | loop fusion | bytes 10485760 | tf_op jit(solution)/shard_map/slice | solution.py:47
  197.2 6.6 %fusion.52 = (f32[16,128]{1,0:T(8,128)S(1)}, f32[16,128,640]{2,1,0:T(8,128)}) fusion(pred[128,640]{1,0:T(8,128)(4,1)} %and_and_fusion, bf16[128,16,128]{0,2,1:T(8,128)(2,1)} %bitcast.124, bf16[640,16,128]{0,2,1:T(8,128)(2,1)} %bitcast.115), kind=kOutput, calls=%fused_computation.110 | convolution fusion | flops 342098560 | bytes 8478720 | tf_op jit(solution)/shard_map/sub | solution.py:71
  213.3 5.3 copy.72
  218.6 6.8 %stack_reshape.7 = f32[5,128,1,2048]{3,1,0,2:T(8,128)} reshape(f32[640,16,128]{2,1,0:T(8,128)} %copy.72) | data formatting | bytes 10485760 | tf_op jit(solution)/shard_map/stack;reshape | solution.py:95
  230.5 7.4 %reshape.152 = f32[5,128,1,2048]{1,0,3,2:T(8,128)} reshape(f32[640,16,128]{0,2,1:T(8,128)} %convolution_bitcast_fusion) | data formatting | bytes 10485760 | tf_op jit(solution)/shard_map/stack;reshape | solution.py:95
  237.8 7.9 %copy.73 = f32[5,128,1,2048]{3,1,2,0:T(8,128)} copy(f32[5,128,1,2048]{1,0,3,2:T(8,128)} %reshape.152) | data formatting | bytes 10485760 | tf_op jit(solution)/shard_map/stack;reshape | solution.py:95
  249.1 44.7 %collective-permute-done.5 = f32[128,2,2048]{2,0,1:T(8,128)S(1)} collective-permute-done((f32[128,2,2048]{2,0,1:T(8,128)S(1)}, f32[128,2,2048]{2,0,1:T(8,128)S(1)}, u32[]{:S(2)}, u32[]{:S(2)}) %collective-permute-start.5) | collective-permute-done | bytes 2097184 | tf_op jit(solution)/shard_map/ppermute | solution.py:15
  295.7 44.1 %collective-permute-done.6 = f32[128,2,2048]{2,0,1:T(8,128)S(1)} collective-permute-done((f32[128,2,2048]{2,0,1:T(8,128)S(1)}, f32[128,2,2048]{2,0,1:T(8,128)S(1)}, u32[]{:S(2)}, u32[]{:S(2)}) %collective-permute-start.6) | collective-permute-done | bytes 2097184 | tf_op jit(solution)/shard_map/ppermute | solution.py:15
  341.7 42.9 %collective-permute-done.7 = f32[128,2,2048]{2,0,1:T(8,128)S(1)} collective-permute-done((f32[128,2,2048]{2,0,1:T(8,128)S(1)}, f32[128,2,2048]{2,0,1:T(8,128)S(1)}, u32[]{:S(2)}, u32[]{:S(2)}) %collective-permute-start.7) | collective-permute-done | bytes 2097184 | tf_op jit(solution)/shard_map/ppermute | solution.py:15
  392.0 37.3 %collective-permute-done.8 = f32[128,2,2048]{2,0,1:T(8,128)} collective-permute-done((f32[128,2,2048]{2,0,1:T(8,128)}, f32[128,2,2048]{2,0,1:T(8,128)}, u32[]{:S(2)}, u32[]{:S(2)}) %collective-permute-start.8) | collective-permute-done | bytes 2097184 | tf_op jit(solution)/shard_map/ppermute | solution.py:15
  437.5 6.2 %collective-permute-done.9 = f32[6,3,2048]{2,0,1:T(8,128)S(1)} collective-permute-done((f32[6,3,2048]{2,0,1:T(8,128)S(1)}, f32[6,3,2048]{2,0,1:T(8,128)S(1)}, u32[]{:S(2)}, u32[]{:S(2)}) %collective-permute-start.9) | collective-permute-done | bytes 147488 | tf_op jit(solution)/shard_map/ppermute | solution.py:15
  456.3 74.4 %all-reduce.2.cloned.1.call-done = f32[3,7,2048]{2,0,1:T(4,128)} async-done(((f32[3,7,2048]{2,0,1:T(4,128)}), f32[3,7,2048]{2,0,1:T(4,128)}) %all-reduce.2.cloned.1.call-update) | async-done | bytes 172048 | tf_op jit(solution)/shard_map/psum | solution.py:114
  (115 shorter events, 104.4 us)
Async XLA Ops:
  26.2 24.4 %all-to-all-start = ((bf16[4,2,98304]{2,1,0:T(2,128)(2,1)}), bf16[4,2,98304]{2,1,0:T(2,128)(2,1)S(1)}, u32[]{:S(2)}, u32[]{:S(2)}) async-start(bf16[4,2,98304]{2,1,0:T(2,128)(2,1)} %reshape.158), calls=%async_computation | async-start | bytes 3145728 | tf_op jit(solution)/shard_map/all_to_all | solution.py:25
  68.2 6.4 %collective-permute-start = (bf16[6,3,2048]{2,0,1:T(8,128)(2,1)S(1)}, bf16[6,3,2048]{2,0,1:T(8,128)(2,1)S(1)}, u32[]{:S(2)}, u32[]{:S(2)}) collective-permute-start(bf16[6,3,2048]{2,0,1:T(8,128)(2,1)S(1)} %slice.138), channel_id=1, source_target_pairs={{0,4},{4,8},{8,12},{12,16},{16,20},{20,24},{24,28},{1,5},{5,9},{9,... | collective-permute-start | bytes 221192 | tf_op jit(solution)/shard_map/ppermute | solution.py:15
  72.5 6.7 %copy-start.11 = (f32[3,1,2048]{2,0,1:T(4,128)}, f32[3,1,2048]{2,0,1:T(4,128)S(1)}, u32[]{:S(2)}) copy-start(f32[3,1,2048]{2,0,1:T(4,128)S(1)} %copy.107) | copy-start | bytes 73732
  80.4 57.7 %copy-start.17 = (s32[8]{0:T(128)S(1)}, s32[8]{0:T(128)}, u32[]{:S(2)}) copy-start(s32[8]{0:T(128)} %param.6) | copy-start | bytes 100
  81.5 25.4 %collective-permute-start.1 = (bf16[128,2,2048]{2,0,1:T(8,128)(2,1)S(1)}, bf16[128,2,2048]{2,0,1:T(8,128)(2,1)}, u32[]{:S(2)}, u32[]{:S(2)}) collective-permute-start(bf16[128,2,2048]{2,0,1:T(8,128)(2,1)S(1)} %get-tuple-element.24), channel_id=1, source_target_pairs={{0,4},{4,8},{8,12},{12,16},{16,20},{20,24},{24,28},{1,5},{5,9},{9,... | collective-permute-start | bytes 3145736 | tf_op jit(solution)/shard_map/ppermute | solution.py:15
  106.8 24.9 %collective-permute-start.2 = (bf16[128,2,2048]{2,0,1:T(8,128)(2,1)}, bf16[128,2,2048]{2,0,1:T(8,128)(2,1)}, u32[]{:S(2)}, u32[]{:S(2)}) collective-permute-start(bf16[128,2,2048]{2,0,1:T(8,128)(2,1)} %collective-permute-done.1), channel_id=1, source_target_pairs={{0,4},{4,8},{8,12},{12,16},{16,20},{20,24},{24,28},{1,5},{5,9},{9,... | collective-permute-start | bytes 3145736 | tf_op jit(solution)/shard_map/ppermute | solution.py:15
  131.8 24.7 %collective-permute-start.3 = (bf16[128,2,2048]{2,0,1:T(8,128)(2,1)}, bf16[128,2,2048]{2,0,1:T(8,128)(2,1)}, u32[]{:S(2)}, u32[]{:S(2)}) collective-permute-start(bf16[128,2,2048]{2,0,1:T(8,128)(2,1)} %collective-permute-done.2), channel_id=1, source_target_pairs={{0,4},{4,8},{8,12},{12,16},{16,20},{20,24},{24,28},{1,5},{5,9},{9,... | collective-permute-start | bytes 3145736 | tf_op jit(solution)/shard_map/ppermute | solution.py:15
  156.5 23.9 %collective-permute-start.4 = (bf16[128,2,2048]{2,0,1:T(8,128)(2,1)}, bf16[128,2,2048]{2,0,1:T(8,128)(2,1)}, u32[]{:S(2)}, u32[]{:S(2)}) collective-permute-start(bf16[128,2,2048]{2,0,1:T(8,128)(2,1)} %collective-permute-done.3), channel_id=1, source_target_pairs={{0,4},{4,8},{8,12},{12,16},{16,20},{20,24},{24,28},{1,5},{5,9},{9,... | collective-permute-start | bytes 3145736 | tf_op jit(solution)/shard_map/ppermute | solution.py:15
  245.7 48.1 %slice-start = ((s8[5242880]{0:T(1024)(128)(4,1)}), s8[4194304]{0:T(1024)(128)(4,1)S(1)}, s32[]{:S(2)}) async-start(s8[5242880]{0:T(1024)(128)(4,1)} %bitcast.108), calls=%async_computation.3 | async-start | bytes 8388608
  245.7 48.1 %slice-start.1 = ((s8[5242880]{0:T(1024)(128)(4,1)}), s8[1048576]{0:T(1024)(128)(4,1)S(1)}, s32[]{:S(2)}) async-start(s8[5242880]{0:T(1024)(128)(4,1)} %bitcast.108), calls=%async_computation.4 | async-start | bytes 2097152
  245.7 48.1 %copy-start = (f32[5,128,1,2048]{3,1,2,0:T(8,128)S(1)}, f32[5,128,1,2048]{3,1,2,0:T(8,128)}, u32[]{:S(2)}) copy-start(f32[5,128,1,2048]{3,1,2,0:T(8,128)} %copy.73) | copy-start | bytes 15728644
  247.5 46.3 %collective-permute-start.5 = (f32[128,2,2048]{2,0,1:T(8,128)S(1)}, f32[128,2,2048]{2,0,1:T(8,128)S(1)}, u32[]{:S(2)}, u32[]{:S(2)}) collective-permute-start(f32[128,2,2048]{2,0,1:T(8,128)S(1)} %fusion.25), channel_id=1, source_target_pairs={{4,0},{8,4},{12,8},{16,12},{20,16},{24,20},{28,24},{5,1},{9,5},{13... | collective-permute-start | bytes 6291464 | tf_op jit(solution)/shard_map/ppermute | solution.py:15
  294.2 45.6 %collective-permute-start.6 = (f32[128,2,2048]{2,0,1:T(8,128)S(1)}, f32[128,2,2048]{2,0,1:T(8,128)S(1)}, u32[]{:S(2)}, u32[]{:S(2)}) collective-permute-start(f32[128,2,2048]{2,0,1:T(8,128)S(1)} %fusion.28), channel_id=1, source_target_pairs={{4,0},{8,4},{12,8},{16,12},{20,16},{24,20},{28,24},{5,1},{9,5},{13... | collective-permute-start | bytes 6291464 | tf_op jit(solution)/shard_map/ppermute | solution.py:15
  340.1 47.3 %copy-start.2 = (bf16[640,1,2048]{0,2,1:T(8,128)(2,1)S(1)}, bf16[640,1,2048]{0,2,1:T(8,128)(2,1)}, u32[]{:S(2)}) copy-start(bf16[640,1,2048]{0,2,1:T(8,128)(2,1)} %copy.62) | copy-start | bytes 7864324
  340.1 47.3 %copy-start.3 = (bf16[16,128,640]{2,1,0:T(8,128)(2,1)S(1)}, bf16[16,128,640]{2,1,0:T(8,128)(2,1)}, u32[]{:S(2)}) copy-start(bf16[16,128,640]{2,1,0:T(8,128)(2,1)} %fusion.2) | copy-start | bytes 7864324
  340.1 44.4 %collective-permute-start.7 = (f32[128,2,2048]{2,0,1:T(8,128)S(1)}, f32[128,2,2048]{2,0,1:T(8,128)S(1)}, u32[]{:S(2)}, u32[]{:S(2)}) collective-permute-start(f32[128,2,2048]{2,0,1:T(8,128)S(1)} %fusion.31), channel_id=1, source_target_pairs={{4,0},{8,4},{12,8},{16,12},{20,16},{24,20},{28,24},{5,1},{9,5},{13... | collective-permute-start | bytes 6291464 | tf_op jit(solution)/shard_map/ppermute | solution.py:15
  386.1 43.2 %collective-permute-start.8 = (f32[128,2,2048]{2,0,1:T(8,128)}, f32[128,2,2048]{2,0,1:T(8,128)}, u32[]{:S(2)}, u32[]{:S(2)}) collective-permute-start(f32[128,2,2048]{2,0,1:T(8,128)} %fusion.23), channel_id=1, source_target_pairs={{4,0},{8,4},{12,8},{16,12},{20,16},{24,20},{28,24},{5,1},{9,5},{13... | collective-permute-start | bytes 6291464 | tf_op jit(solution)/shard_map/ppermute | solution.py:15
  392.0 39.8 %copy-start.1 = (f32[128,1,2048]{2,0,1:T(8,128)S(1)}, f32[128,1,2048]{2,0,1:T(8,128)}, u32[]{:S(2)}) copy-start(f32[128,1,2048]{2,0,1:T(8,128)} %copy.75) | copy-start | bytes 3145732
  435.5 8.3 %collective-permute-start.9 = (f32[6,3,2048]{2,0,1:T(8,128)S(1)}, f32[6,3,2048]{2,0,1:T(8,128)S(1)}, u32[]{:S(2)}, u32[]{:S(2)}) collective-permute-start(f32[6,3,2048]{2,0,1:T(8,128)S(1)} %fusion.45), channel_id=1, source_target_pairs={{4,0},{8,4},{12,8},{16,12},{20,16},{24,20},{28,24},{5,1},{9,5},{13... | collective-permute-start | bytes 442376 | tf_op jit(solution)/shard_map/ppermute | solution.py:15
  437.5 6.6 %copy-start.12 = (f32[3,1,2048]{2,0,1:T(4,128)S(1)}, f32[3,1,2048]{2,0,1:T(4,128)}, u32[]{:S(2)}) copy-start(f32[3,1,2048]{2,0,1:T(4,128)} %copy-done.11) | copy-start | bytes 73732
  446.8 7.2 %copy-start.15 = (f32[3,2048]{1,0:T(4,128)S(1)}, f32[3,2048]{1,0:T(4,128)}, u32[]{:S(2)}) copy-start(f32[3,2048]{1,0:T(4,128)} %get-tuple-element.16) | copy-start | bytes 73732
  446.8 7.8 %copy-start.14 = (f32[3,2048]{1,0:T(4,128)S(1)}, f32[3,2048]{1,0:T(4,128)}, u32[]{:S(2)}) copy-start(f32[3,2048]{1,0:T(4,128)} %get-tuple-element.15) | copy-start | bytes 73732
  449.5 82.8 %all-to-all-start.1 = ((bf16[128,3,2048]{2,1,0:T(4,128)(2,1)}), bf16[128,3,2048]{2,1,0:T(4,128)(2,1)S(1)}, u32[]{:S(2)}, u32[]{:S(2)}) async-start(bf16[128,3,2048]{2,1,0:T(4,128)(2,1)} %copy.76), calls=%async_computation.1 | async-start | bytes 4194304 | tf_op jit(solution)/shard_map/all_to_all | solution.py:115
  453.3 77.4 %all-reduce.2.cloned.1.call-start = ((), (), s32[]{:S(2)}) async-start(), calls=%async_computation.2 | async-start | bytes 458752 | tf_op jit(solution)/shard_map/psum | solution.py:114
  (9 other events, 36.9 us)
Sparse Core Ops, SparseCore 0:
  458.1 72.5 all-reduce.1
where the time goes:
time: 544 us; the launch traced here: 542 us
  waiting for transfers between devices  328 us (60%)
  local copies, waits for them, and re-layouts  114 us (21%)
  starting transfers between devices  42.9 us (8%)
  matrix products  22.2 us (4%)
  other arithmetic  20.2 us (4%)
  between operations  14.5 us (3%)
    ppermute x10, waiting for transfers between devices, from_behind(): lax.ppermute(value, axis, [(source, source + steps) for source in range(f...  234 us
    psum x1, waiting for transfers between devices, shards(): filter_grad = lax.psum(tap_terms, 'ctx')  74.4 us
    unnamed x63, local copies, waits for them, and re-layouts  44.5 us
    ppermute x10, starting transfers between devices, from_behind(): lax.ppermute(value, axis, [(source, source + steps) for source in range(f...  34.8 us
    another operation x3, local copies, waits for them, and re-layouts, shards(): jnp.stack([key_part.reshape(reach, tokens, width), value_part.reshape(rea...  22 us
    all_to_all x1, waiting for transfers between devices, shards(): local = lax.all_to_all(qkv, 'tp', split_axis=2, concat_axis=0, tiled=True)  19.9 us
  transfers between devices with their start and end apart: 13, of which 12 were waited for; matrix products, arithmetic and copies ran while one was open for 5% of the time, Pallas kernels for 0%

commit v1 on v0

--- a/solution.py
+++ b/solution.py
@@ -22,7 +22,19 @@
 
 
 def shards(qkv, filters, doc_ids, upstream):
-    local = lax.all_to_all(qkv, "tp", split_axis=2, concat_axis=0, tiled=True)
+    ways, here = (lax.axis_size("tp"), lax.axis_index("tp"))
+    width_2 = qkv.shape[2] // ways
+    dims = list(qkv.shape)
+    dims[2] = width_2
+    height = dims[0]
+    dims[0] = height * ways
+    full = jnp.zeros(dims, qkv.dtype)
+    for mask in range(ways):
+        part = lax.dynamic_slice_in_dim(qkv, (here ^ mask) * width_2, width_2, axis=2)
+        if mask:
+            part = lax.ppermute(part, "tp", [(d, d ^ mask) for d in range(ways)])
+        full = lax.dynamic_update_slice_in_dim(full, part, (here ^ mask) * height, axis=0)
+    local = full
     tokens = local.shape[0]
     width = local.shape[2]
     heads = width // HEAD_DIM

time: 544 us -> 572 us (1.051)
  other arithmetic: 20.2 us -> 56.4 us
  local copies, waits for them, and re-layouts: 114 us -> 122 us
  waiting for transfers between devices: 328 us -> 321 us
    dynamic_update_slice x0 -> x4, local copies, waits for them, and re-layouts: none -> 39.4 us  [shards(): lax.dynamic_update_slice_in_dim(full, part, (here ^ mask) * height, axis=0)]
    unnamed x63 -> x83, local copies, waits for them, and re-layouts: 44.5 us -> 19.1 us
    reduce_sum x1, other arithmetic: 3.59 us -> 25 us  [shards(): jnp.sum(inputs[KW - 1 - lag:KW - 1 - lag + tokens] * conv_grad, axis=0)]
    all_to_all x1 -> x0, waiting for transfers between devices: 19.9 us -> none  [shards(): local = lax.all_to_all(qkv, 'tp', split_axis=2, concat_axis=0, tiled=True)]
    ppermute x10, waiting for transfers between devices: 234 us -> 245 us  [from_behind(): lax.ppermute(value, axis, [(source, source + steps) for source in range(f...]
    all_to_all x1 -> x0, local copies, waits for them, and re-layouts: 10.5 us -> none  [shards(): local = lax.all_to_all(qkv, 'tp', split_axis=2, concat_axis=0, tiled=True)]
    convert_element_type x1, other arithmetic: 2.64 us -> 12.4 us  [shards(): input_grad.astype(jnp.bfloat16)]
    convert_element_type x1, other arithmetic: 2.64 us -> 11.8 us  [shards(): mixed = mixed.astype(jnp.bfloat16)]
  transfers between devices with their start and end apart: 13 -> 15, of which waited for: 12 -> 11; matrix products, arithmetic and copies ran while one was open for 5% -> 9% of each run, Pallas kernels for 0% -> 0%
where the time goes in v1:
time: 572 us; the launch traced here: 571 us
  waiting for transfers between devices  321 us (56%)
  local copies, waits for them, and re-layouts  122 us (21%)
  other arithmetic  56.4 us (10%)
  starting transfers between devices  39.9 us (7%)
  matrix products  17.5 us (3%)
  between operations  14.7 us (3%)
    ppermute x10, waiting for transfers between devices, from_behind(): lax.ppermute(value, axis, [(source, source + steps) for source in range(f...  245 us
    psum x1, waiting for transfers between devices, shards(): filter_grad = lax.psum(tap_terms, 'ctx')  75.5 us
    dynamic_update_slice x4, local copies, waits for them, and re-layouts, shards(): lax.dynamic_update_slice_in_dim(full, part, (here ^ mask) * height, axis=0)  39.4 us
    ppermute x10, starting transfers between devices, from_behind(): lax.ppermute(value, axis, [(source, source + steps) for source in range(f...  33 us
    reduce_sum x1, other arithmetic, shards(): jnp.sum(inputs[KW - 1 - lag:KW - 1 - lag + tokens] * conv_grad, axis=0)  25 us
    another operation x4, local copies, waits for them, and re-layouts, shards(): jnp.stack([key_part.reshape(reach, tokens, width), value_part.reshape(rea...  24.6 us
    unnamed x83, local copies, waits for them, and re-layouts  19.1 us
    convert_element_type x1, other arithmetic, shards(): input_grad.astype(jnp.bfloat16)  12.4 us
  transfers between devices with their start and end apart: 15, of which 11 were waited for; matrix products, arithmetic and copies ran while one was open for 9% of the time, Pallas kernels for 0%

profile of v1, /device:TPU:0, one launch (start us, length us, event | category | flops | bytes accessed | tf_op | source)
XLA Modules:
  0.0 570.9 jit_solution(11901681186360844059)
XLA Ops:
  15.1 6.1 %dynamic_update_slice.12 = bf16[128,3,2048]{0,2,1:T(8,128)(2,1)S(1)} dynamic-update-slice(bf16[128,3,2048]{0,2,1:T(8,128)(2,1)S(1)} %broadcast_in_dim.20, bf16[32,3,2048]{0,2,1:T(8,128)(2,1)S(1)} %copy.102, s32[]{:T(128)S(6)} %select_n.38, s32[]{:T(128)} %constant.13.clone.1, s32[]{:T(128)} %constant.13.clone.1) | dynamic-update-slice | bytes 786436 | tf_op jit(solution)/shard_map/dynamic_update_slice | solution.py:36
  24.4 11.1 %dynamic_update_slice.13 = bf16[128,3,2048]{0,2,1:T(8,128)(2,1)S(1)} dynamic-update-slice(bf16[128,3,2048]{0,2,1:T(8,128)(2,1)S(1)} %dynamic_update_slice.12, bf16[32,3,2048]{0,2,1:T(8,128)(2,1)S(1)} %copy.62, s32[]{:T(128)S(6)} %select_n.40, s32[]{:T(128)} %constant.13.clone.1, s32[]{:T(128)} %constant.13.clone.1) | dynamic-update-slice | bytes 786436 | tf_op jit(solution)/shard_map/dynamic_update_slice | solution.py:36
  37.2 11.1 %dynamic_update_slice.14 = bf16[128,3,2048]{0,2,1:T(8,128)(2,1)S(1)} dynamic-update-slice(bf16[128,3,2048]{0,2,1:T(8,128)(2,1)S(1)} %dynamic_update_slice.13, bf16[32,3,2048]{0,2,1:T(8,128)(2,1)S(1)} %copy.63, s32[]{:T(128)S(6)} %select_n.42, s32[]{:T(128)} %constant.13.clone.1, s32[]{:T(128)} %constant.13.clone.1) | dynamic-update-slice | bytes 786436 | tf_op jit(solution)/shard_map/dynamic_update_slice | solution.py:36
  50.0 11.1 %dynamic_update_slice.15 = bf16[128,3,2048]{0,2,1:T(8,128)(2,1)S(1)} dynamic-update-slice(bf16[128,3,2048]{0,2,1:T(8,128)(2,1)S(1)} %dynamic_update_slice.14, bf16[32,3,2048]{0,2,1:T(8,128)(2,1)S(1)} %copy.64, s32[]{:T(128)S(6)} %select_n.44, s32[]{:T(128)} %constant.13.clone.1, s32[]{:T(128)} %constant.13.clone.1) | dynamic-update-slice | bytes 786436 | tf_op jit(solution)/shard_map/dynamic_update_slice | solution.py:36
  70.7 11.8 %add_convert_fusion = bf16[128,3,2048]{0,2,1:T(8,128)(2,1)S(1)} fusion(f32[134,3,2048]{0,2,1:T(8,128)S(1)} %maximum_convert_fusion, f32[3,2048]{1,0:T(4,128)S(1)} %get-tuple-element.48, f32[3,2048]{1,0:T(4,128)S(1)} %get-tuple-element.49, f32[3,2048]{1,0:T(4,128)S(1)} %copy-done.12, f32[3,2048]{1,0:T(4,128)S(1)} %copy-done.13, f32[3,2048]{1,0:T(4,128)S(1)} %copy-done.14, ...), kind=kLoop, calls=%fused_computation.41 | loop fusion | flops 11010048 | bytes 23764992 | tf_op jit(solution)/shard_map/convert_element_type | solution.py:50
  88.3 21.1 %collective-permute-done.4 = bf16[128,2,2048]{0,2,1:T(8,128)(2,1)S(1)} collective-permute-done((bf16[128,2,2048]{0,2,1:T(8,128)(2,1)S(1)}, bf16[128,2,2048]{0,2,1:T(8,128)(2,1)S(1)}, u32[]{:S(2)}, u32[]{:S(2)}) %collective-permute-start.4) | collective-permute-done | bytes 1048608 | tf_op jit(solution)/shard_map/ppermute | solution.py:15
  109.3 5.5 collective-permute-start.5
  114.8 19.1 %collective-permute-done.5 = bf16[128,2,2048]{0,2,1:T(8,128)(2,1)} collective-permute-done((bf16[128,2,2048]{0,2,1:T(8,128)(2,1)S(1)}, bf16[128,2,2048]{0,2,1:T(8,128)(2,1)}, u32[]{:S(2)}, u32[]{:S(2)}) %collective-permute-start.5) | collective-permute-done | bytes 1048608 | tf_op jit(solution)/shard_map/ppermute | solution.py:15
  133.9 6.2 %collective-permute-start.6 = (bf16[128,2,2048]{0,2,1:T(8,128)(2,1)}, bf16[128,2,2048]{0,2,1:T(8,128)(2,1)}, u32[]{:S(2)}, u32[]{:S(2)}) collective-permute-start(bf16[128,2,2048]{0,2,1:T(8,128)(2,1)} %collective-permute-done.5), channel_id=1, source_target_pairs={{0,4},{4,8},{8,12},{12,16},{16,20},{20,24},{24,28},{1,5},{5,9},{9,... | collective-permute-start | bytes 3145736 | tf_op jit(solution)/shard_map/ppermute | solution.py:15
  144.0 14.7 %collective-permute-done.6 = bf16[128,2,2048]{0,2,1:T(8,128)(2,1)} collective-permute-done((bf16[128,2,2048]{0,2,1:T(8,128)(2,1)}, bf16[128,2,2048]{0,2,1:T(8,128)(2,1)}, u32[]{:S(2)}, u32[]{:S(2)}) %collective-permute-start.6) | collective-permute-done | bytes 1048608 | tf_op jit(solution)/shard_map/ppermute | solution.py:15
  158.8 6.3 %collective-permute-start.7 = (bf16[128,2,2048]{0,2,1:T(8,128)(2,1)}, bf16[128,2,2048]{0,2,1:T(8,128)(2,1)}, u32[]{:S(2)}, u32[]{:S(2)}) collective-permute-start(bf16[128,2,2048]{0,2,1:T(8,128)(2,1)} %collective-permute-done.6), channel_id=1, source_target_pairs={{0,4},{4,8},{8,12},{12,16},{16,20},{20,24},{24,28},{1,5},{5,9},{9,... | collective-permute-start | bytes 3145736 | tf_op jit(solution)/shard_map/ppermute | solution.py:15
  172.7 10.1 %collective-permute-done.7 = bf16[128,2,2048]{0,2,1:T(8,128)(2,1)} collective-permute-done((bf16[128,2,2048]{0,2,1:T(8,128)(2,1)}, bf16[128,2,2048]{0,2,1:T(8,128)(2,1)}, u32[]{:S(2)}, u32[]{:S(2)}) %collective-permute-start.7) | collective-permute-done | bytes 1048608 | tf_op jit(solution)/shard_map/ppermute | solution.py:15
  202.9 5.3 copy.76
  208.2 6.8 %stack_reshape.7 = f32[5,128,1,2048]{3,1,0,2:T(8,128)} reshape(f32[640,16,128]{2,1,0:T(8,128)} %copy.76) | data formatting | bytes 10485760 | tf_op jit(solution)/shard_map/stack;reshape | solution.py:107
  214.9 5.9 %copy.78 = f32[5,128,1,2048]{1,3,2,0:T(8,128)} copy(f32[5,128,1,2048]{3,1,0,2:T(8,128)} %stack_reshape.7) | data formatting | bytes 10485760 | tf_op jit(solution)/shard_map/stack;reshape | solution.py:107
  224.0 7.4 %reshape.152 = f32[5,128,1,2048]{1,0,3,2:T(8,128)} reshape(f32[640,16,128]{0,2,1:T(8,128)} %convolution_bitcast_fusion) | data formatting | bytes 10485760 | tf_op jit(solution)/shard_map/stack;reshape | solution.py:107
  237.5 44.7 %collective-permute-done.8 = f32[128,2,2048]{0,2,1:T(8,128)S(1)} collective-permute-done((f32[128,2,2048]{0,2,1:T(8,128)S(1)}, f32[128,2,2048]{0,2,1:T(8,128)S(1)}, u32[]{:S(2)}, u32[]{:S(2)}) %collective-permute-start.8) | collective-permute-done | bytes 2097184 | tf_op jit(solution)/shard_map/ppermute | solution.py:15
  283.6 44.4 %collective-permute-done.9 = f32[128,2,2048]{0,2,1:T(8,128)S(1)} collective-permute-done((f32[128,2,2048]{0,2,1:T(8,128)S(1)}, f32[128,2,2048]{0,2,1:T(8,128)S(1)}, u32[]{:S(2)}, u32[]{:S(2)}) %collective-permute-start.9) | collective-permute-done | bytes 2097184 | tf_op jit(solution)/shard_map/ppermute | solution.py:15
  329.8 44.4 %collective-permute-done.10 = f32[128,2,2048]{0,2,1:T(8,128)S(1)} collective-permute-done((f32[128,2,2048]{0,2,1:T(8,128)S(1)}, f32[128,2,2048]{0,2,1:T(8,128)S(1)}, u32[]{:S(2)}, u32[]{:S(2)}) %collective-permute-start.10) | collective-permute-done | bytes 2097184 | tf_op jit(solution)/shard_map/ppermute | solution.py:15
  377.8 39.7 %collective-permute-done.11 = f32[128,2,2048]{0,2,1:T(8,128)S(1)} collective-permute-done((f32[128,2,2048]{0,2,1:T(8,128)S(1)}, f32[128,2,2048]{0,2,1:T(8,128)S(1)}, u32[]{:S(2)}, u32[]{:S(2)}) %collective-permute-start.11) | collective-permute-done | bytes 2097184 | tf_op jit(solution)/shard_map/ppermute | solution.py:15
  417.9 25.0 %multiply_reduce_fusion = (f32[3,2048]{1,0:T(4,128)}, f32[3,2048]{1,0:T(4,128)}, f32[3,2048]{1,0:T(4,128)}, f32[3,2048]{1,0:T(4,128)}, f32[3,2048]{1,0:T(4,128)}, /*index=5*/f32[3,2048]{1,0:T(4,128)}, f32[3,2048]{1,0:T(4,128)}) fusion(f32[134,3,2048]{0,2,1:T(8,128)} %copy-done, f32[128,2,2048]{0,2,1:T(8,128)S(1)} %fusion.34, f32[128,1,2048]{0,2,1:T(8,128)} %bitcast.100), kind=kLoop, calls=%fused_computation.34 | loop fusion | flops 11753472 | bytes 25337856 | tf_op jit(solution)/shard_map/reduce_sum | solution.py:121
  451.3 5.0 collective-permute-done.12
  461.9 12.4 %fusion.6 = bf16[128,3,2048]{0,2,1:T(8,128)(2,1)} fusion(f32[134,3,2048]{0,2,1:T(8,128)S(1)} %pad_maximum_fusion, f32[3,2048]{1,0:T(4,128)S(1)} %get-tuple-element.48, f32[3,2048]{1,0:T(4,128)S(1)} %copy-done.17, f32[3,2048]{1,0:T(4,128)S(1)} %copy-done.12, f32[3,2048]{1,0:T(4,128)S(1)} %copy-done.13, f32[3,2048]{1,0:T(4,128)S(1)} %copy-done.14, ...), kind=kLoop, calls=%fused_computation.22 | loop fusion | flops 11796480 | bytes 23764992 | tf_op jit(solution)/shard_map/convert_element_type | solution.py:128
  484.5 75.5 %all-reduce.2.cloned.1.call-done = f32[3,7,2048]{2,0,1:T(4,128)} async-done(((f32[3,7,2048]{2,0,1:T(4,128)}), f32[3,7,2048]{2,0,1:T(4,128)}) %all-reduce.2.cloned.1.call-update) | async-done | bytes 172048 | tf_op jit(solution)/shard_map/psum | solution.py:126
  (148 shorter events, 105.4 us)
Async XLA Ops:
  9.6 38.7 %collective-permute-start.2 = (bf16[32,3,2048]{2,0,1:T(8,128)(2,1)S(1)}, bf16[32,3,2048]{2,0,1:T(8,128)(2,1)}, u32[]{:S(2)}, u32[]{:S(2)}) collective-permute-start(bf16[32,3,2048]{2,0,1:T(8,128)(2,1)S(1)} %get-tuple-element.26), channel_id=1, source_target_pairs={{0,3},{1,2},{2,1},{3,0},{4,7},{5,6},{6,5},{7,4},{8,11},{9,10},{10,... | collective-permute-start | bytes 1179656 | tf_op jit(solution)/shard_map/ppermute | solution.py:35
  12.0 10.7 %collective-permute-start = (bf16[32,3,2048]{2,0,1:T(8,128)(2,1)}, bf16[32,3,2048]{2,0,1:T(8,128)(2,1)}, u32[]{:S(2)}, u32[]{:S(2)}) collective-permute-start(bf16[32,3,2048]{2,0,1:T(8,128)(2,1)} %get-tuple-element.27), channel_id=1, source_target_pairs={{0,1},{1,0},{2,3},{3,2},{4,5},{5,4},{6,7},{7,6},{8,9},{9,8},{10,11... | collective-permute-start | bytes 1179656 | tf_op jit(solution)/shard_map/ppermute | solution.py:35
  12.7 22.8 %collective-permute-start.1 = (bf16[32,3,2048]{2,0,1:T(8,128)(2,1)}, bf16[32,3,2048]{2,0,1:T(8,128)(2,1)}, u32[]{:S(2)}, u32[]{:S(2)}) collective-permute-start(bf16[32,3,2048]{2,0,1:T(8,128)(2,1)} %get-tuple-element.29), channel_id=1, source_target_pairs={{0,2},{1,3},{2,0},{3,1},{4,6},{5,7},{6,4},{7,5},{8,10},{9,11},{10,... | collective-permute-start | bytes 1179656 | tf_op jit(solution)/shard_map/ppermute | solution.py:35
  62.4 6.2 %collective-permute-start.3 = (bf16[6,3,2048]{2,0,1:T(8,128)(2,1)S(1)}, bf16[6,3,2048]{2,0,1:T(8,128)(2,1)S(1)}, u32[]{:S(2)}, u32[]{:S(2)}) collective-permute-start(bf16[6,3,2048]{2,0,1:T(8,128)(2,1)S(1)} %copy.65), channel_id=1, source_target_pairs={{0,4},{4,8},{8,12},{12,16},{16,20},{20,24},{24,28},{1,5},{5,9},{9,... | collective-permute-start | bytes 221192 | tf_op jit(solution)/shard_map/ppermute | solution.py:15
  70.6 11.9 %copy-start = (f32[134,3,2048]{0,2,1:T(8,128)}, f32[134,3,2048]{0,2,1:T(8,128)S(1)}, u32[]{:S(2)}) copy-start(f32[134,3,2048]{0,2,1:T(8,128)S(1)} %maximum_convert_fusion) | copy-start | bytes 9879556
  82.5 57.6 %copy-start.28 = (s32[8]{0:T(128)S(1)}, s32[8]{0:T(128)}, u32[]{:S(2)}) copy-start(s32[8]{0:T(128)} %param.6) | copy-start | bytes 100
  82.5 83.2 %copy-start.10 = (bf16[128,2048]{1,0:T(8,128)(2,1)S(1)}, bf16[128,2048]{1,0:T(8,128)(2,1)}, u32[]{:S(2)}) copy-start(bf16[128,2048]{1,0:T(8,128)(2,1)} %param.7) | copy-start | bytes 1572868
  83.9 25.4 %collective-permute-start.4 = (bf16[128,2,2048]{0,2,1:T(8,128)(2,1)S(1)}, bf16[128,2,2048]{0,2,1:T(8,128)(2,1)S(1)}, u32[]{:S(2)}, u32[]{:S(2)}) collective-permute-start(bf16[128,2,2048]{0,2,1:T(8,128)(2,1)S(1)} %get-tuple-element.24), channel_id=1, source_target_pairs={{0,4},{4,8},{8,12},{12,16},{16,20},{20,24},{24,28},{1,5},{5,9},{9,... | collective-permute-start | bytes 3145736 | tf_op jit(solution)/shard_map/ppermute | solution.py:15
  109.3 24.6 %collective-permute-start.5 = (bf16[128,2,2048]{0,2,1:T(8,128)(2,1)S(1)}, bf16[128,2,2048]{0,2,1:T(8,128)(2,1)}, u32[]{:S(2)}, u32[]{:S(2)}) collective-permute-start(bf16[128,2,2048]{0,2,1:T(8,128)(2,1)S(1)} %collective-permute-done.4), channel_id=1, source_target_pairs={{0,4},{4,8},{8,12},{12,16},{16,20},{20,24},{24,28},{1,5},{5,9},{9,... | collective-permute-start | bytes 3145736 | tf_op jit(solution)/shard_map/ppermute | solution.py:15
  133.9 24.8 %collective-permute-start.6 = (bf16[128,2,2048]{0,2,1:T(8,128)(2,1)}, bf16[128,2,2048]{0,2,1:T(8,128)(2,1)}, u32[]{:S(2)}, u32[]{:S(2)}) collective-permute-start(bf16[128,2,2048]{0,2,1:T(8,128)(2,1)} %collective-permute-done.5), channel_id=1, source_target_pairs={{0,4},{4,8},{8,12},{12,16},{16,20},{20,24},{24,28},{1,5},{5,9},{9,... | collective-permute-start | bytes 3145736 | tf_op jit(solution)/shard_map/ppermute | solution.py:15
  158.8 24.1 %collective-permute-start.7 = (bf16[128,2,2048]{0,2,1:T(8,128)(2,1)}, bf16[128,2,2048]{0,2,1:T(8,128)(2,1)}, u32[]{:S(2)}, u32[]{:S(2)}) collective-permute-start(bf16[128,2,2048]{0,2,1:T(8,128)(2,1)} %collective-permute-done.6), channel_id=1, source_target_pairs={{0,4},{4,8},{8,12},{12,16},{16,20},{20,24},{24,28},{1,5},{5,9},{9,... | collective-permute-start | bytes 3145736 | tf_op jit(solution)/shard_map/ppermute | solution.py:15
  202.9 18.0 %copy-start.4 = (bf16[16,128,640]{2,1,0:T(8,128)(2,1)}, bf16[16,128,640]{2,1,0:T(8,128)(2,1)S(1)}, u32[]{:S(2)}) copy-start(bf16[16,128,640]{2,1,0:T(8,128)(2,1)S(1)} %fusion.2) | copy-start | bytes 7864324
  224.0 12.0 %slice-start = ((s8[5242880]{0:T(1024)(128)(4,1)}), s8[1048576]{0:T(1024)(128)(4,1)S(1)}, s32[]{:S(2)}) async-start(s8[5242880]{0:T(1024)(128)(4,1)} %bitcast.98), calls=%async_computation.2 | async-start | bytes 2097152
  236.2 46.0 %collective-permute-start.8 = (f32[128,2,2048]{0,2,1:T(8,128)S(1)}, f32[128,2,2048]{0,2,1:T(8,128)S(1)}, u32[]{:S(2)}, u32[]{:S(2)}) collective-permute-start(f32[128,2,2048]{0,2,1:T(8,128)S(1)} %fusion.26), channel_id=1, source_target_pairs={{4,0},{8,4},{12,8},{16,12},{20,16},{24,20},{28,24},{5,1},{9,5},{13... | collective-permute-start | bytes 6291464 | tf_op jit(solution)/shard_map/ppermute | solution.py:15
  282.3 45.7 %collective-permute-start.9 = (f32[128,2,2048]{0,2,1:T(8,128)S(1)}, f32[128,2,2048]{0,2,1:T(8,128)S(1)}, u32[]{:S(2)}, u32[]{:S(2)}) collective-permute-start(f32[128,2,2048]{0,2,1:T(8,128)S(1)} %fusion.29), channel_id=1, source_target_pairs={{4,0},{8,4},{12,8},{16,12},{20,16},{24,20},{28,24},{5,1},{9,5},{13... | collective-permute-start | bytes 6291464 | tf_op jit(solution)/shard_map/ppermute | solution.py:15
  328.2 47.5 %copy-start.3 = (bf16[640,1,2048]{0,2,1:T(8,128)(2,1)S(1)}, bf16[640,1,2048]{0,2,1:T(8,128)(2,1)}, u32[]{:S(2)}) copy-start(bf16[640,1,2048]{0,2,1:T(8,128)(2,1)} %copy-done.2) | copy-start | bytes 7864324
  328.3 47.5 %copy-start.5 = (bf16[16,128,640]{2,1,0:T(8,128)(2,1)S(1)}, bf16[16,128,640]{2,1,0:T(8,128)(2,1)}, u32[]{:S(2)}) copy-start(bf16[16,128,640]{2,1,0:T(8,128)(2,1)} %copy-done.4) | copy-start | bytes 7864324
  328.3 46.0 %collective-permute-start.10 = (f32[128,2,2048]{0,2,1:T(8,128)S(1)}, f32[128,2,2048]{0,2,1:T(8,128)S(1)}, u32[]{:S(2)}, u32[]{:S(2)}) collective-permute-start(f32[128,2,2048]{0,2,1:T(8,128)S(1)} %fusion.32), channel_id=1, source_target_pairs={{4,0},{8,4},{12,8},{16,12},{20,16},{24,20},{28,24},{5,1},{9,5},{13... | collective-permute-start | bytes 6291464 | tf_op jit(solution)/shard_map/ppermute | solution.py:15
  374.5 43.1 %collective-permute-start.11 = (f32[128,2,2048]{0,2,1:T(8,128)S(1)}, f32[128,2,2048]{0,2,1:T(8,128)S(1)}, u32[]{:S(2)}, u32[]{:S(2)}) collective-permute-start(f32[128,2,2048]{0,2,1:T(8,128)S(1)} %fusion.24), channel_id=1, source_target_pairs={{4,0},{8,4},{12,8},{16,12},{20,16},{24,20},{28,24},{5,1},{9,5},{13... | collective-permute-start | bytes 6291464 | tf_op jit(solution)/shard_map/ppermute | solution.py:15
  417.9 25.0 %copy-start.1 = (f32[16,128,128]{2,1,0:T(8,128)S(1)}, f32[16,128,128]{2,1,0:T(8,128)}, u32[]{:S(2)}) copy-start(f32[16,128,128]{2,1,0:T(8,128)} %fusion.53) | copy-start | bytes 3145732
  447.7 8.7 %collective-permute-start.12 = (f32[6,3,2048]{2,0,1:T(8,128)}, f32[6,3,2048]{2,0,1:T(8,128)}, u32[]{:S(2)}, u32[]{:S(2)}) collective-permute-start(f32[6,3,2048]{2,0,1:T(8,128)} %copy.79), channel_id=1, source_target_pairs={{4,0},{8,4},{12,8},{16,12},{20,16},{24,20},{28,24},{5,1},{9,5},{13... | collective-permute-start | bytes 442376 | tf_op jit(solution)/shard_map/ppermute | solution.py:15
  474.3 8.4 %copy-start.21 = (f32[3,2048]{1,0:T(4,128)S(1)}, f32[3,2048]{1,0:T(4,128)}, u32[]{:S(2)}) copy-start(f32[3,2048]{1,0:T(4,128)} %get-tuple-element.15) | copy-start | bytes 73732
  478.9 82.8 %all-to-all-start = ((bf16[128,3,2048]{2,1,0:T(4,128)(2,1)}), bf16[128,3,2048]{2,1,0:T(4,128)(2,1)S(1)}, u32[]{:S(2)}, u32[]{:S(2)}) async-start(bf16[128,3,2048]{2,1,0:T(4,128)(2,1)} %copy.81), calls=%async_computation | async-start | bytes 4194304 | tf_op jit(solution)/shard_map/all_to_all | solution.py:127
  482.6 77.3 %all-reduce.2.cloned.1.call-start = ((), (), s32[]{:S(2)}) async-start(), calls=%async_computation.1 | async-start | bytes 458752 | tf_op jit(solution)/shard_map/psum | solution.py:126
  (22 other events, 86.6 us)
Sparse Core Ops, SparseCore 0:
  487.4 72.5 all-reduce.1
